TPU v7x, 32 devices: a whole 2x2x4 slice. The times are simulated.
32 devices in a mesh: fsdp: 4 (over y, x), ctx: 4 (over z), tp: 2 (over core).
Axes of the slice: x: 2, y: 2, z: 4, core: 2. Of those that a mesh axis runs over, the one named last changes fastest.
Arguments:
- tokens: bfloat16 [8, 1024, 2048], P('fsdp', 'ctx'), may hold values from -6 to 6
- cotangent: bfloat16 [8, 1024, 2048], P('fsdp', 'ctx'), may hold values from -6 to 6
- prefix_len: int32 [8], P('fsdp'), may hold values from 102 to 512
- group_order: int32 [8], replicated, may hold values from 0 to 7, each once
- ln_gain: bfloat16 [2048], replicated, may hold values from 0.25 to 1.75
- ln_bias: bfloat16 [2048], replicated, may hold values from -4 to 4
- query_weight: bfloat16 [2048, 2048], P('fsdp', 'tp'), may hold values from -0.125 to 0.125
- query_bias: bfloat16 [2048], P('tp'), may hold values from -4 to 4
- key_weight: bfloat16 [2048, 2048], P('fsdp', 'tp'), may hold values from -0.125 to 0.125
- key_bias: bfloat16 [2048], P('tp'), may hold values from -4 to 4
- value_weight: bfloat16 [2048, 2048], P('fsdp', 'tp'), may hold values from -0.125 to 0.125
- value_bias: bfloat16 [2048], P('tp'), may hold values from -4 to 4
- out_weight: bfloat16 [2048, 2048], P('fsdp', 'tp'), may hold values from -1 to 1
- out_bias: bfloat16 [2048], replicated, may hold values from -4 to 4
- up_weight: bfloat16 [2048, 8192], P('fsdp', 'tp'), may hold values from -0.125 to 0.125
- up_bias: bfloat16 [8192], P('tp'), may hold values from -4 to 4
- down_weight: bfloat16 [2048, 8192], P('fsdp', 'tp'), may hold values from -0.0625 to 0.0625
- down_bias: bfloat16 [2048], replicated, may hold values from -4 to 4
Outputs:
- output: bfloat16 [8, 1024, 2048], P('fsdp', 'ctx')
- input_grad: bfloat16 [8, 1024, 2048], P('fsdp', 'ctx')
- ln_gain_grad: float32 [2048], replicated
- ln_bias_grad: float32 [2048], replicated
- query_weight_grad: float32 [2048, 2048], P('fsdp', 'tp')
- query_bias_grad: float32 [2048], P('tp')
- key_weight_grad: float32 [2048, 2048], P('fsdp', 'tp')
- key_bias_grad: float32 [2048], P('tp')
- value_weight_grad: float32 [2048, 2048], P('fsdp', 'tp')
- value_bias_grad: float32 [2048], P('tp')
- out_weight_grad: float32 [2048, 2048], P('fsdp', 'tp')
- up_weight_grad: float32 [2048, 8192], P('fsdp', 'tp')
- up_bias_grad: float32 [8192], P('tp')
- down_weight_grad: float32 [2048, 8192], P('fsdp', 'tp')
- out_biases_grad: float32 [2048], replicated
Inputs may be any that keep to these rules, and one draw needn't show every extreme that they name: Each number of 0 to 7 appears once; storage rows k * 128 to k * 128 + 127 of every sequence hold positions group_order[k] * 128 onwards.
All inputs are finite; a program needn't handle non-finite values.
Results may differ from a plain program's by a relative error of at most 0.012.
Values may be sent and summed in bfloat16 or wider, within the bound.
No kernel may reach another device: no remote copies, remote signals or barrier semaphores. Data moves between devices by JAX's collectives and lax.ppermute only.
A program may use at most 448 MiB of HBM per device.

v0:
```python
import jax
import jax.numpy as jnp
from jax import lax
from jax.sharding import PartitionSpec as P

HD = 64
ROT = 32
SEQ_LEN = 1024
masked_fill = -1e30
norm_eps = 1e-05


def positions(group_order, row_start, row_count, group_len):
    row_index = row_start + jnp.arange(row_count, dtype=jnp.int32)
    slot_index = row_index // group_len
    offset = row_index - slot_index * group_len
    matches = slot_index[:, None] == jnp.arange(group_order.shape[0], dtype=jnp.int32)[None, :]
    anchor = jnp.sum(jnp.where(matches, group_order[None, :], 0), axis=1)
    return anchor * group_len + offset


def rotary_tables(places):
    half_rot = ROT // 2
    frequency = jnp.power(10000.0, -2.0 * jnp.arange(half_rot, dtype=jnp.float32) / ROT)
    angles = places.astype(jnp.float32)[:, None] * frequency[None, :]
    return (jnp.cos(angles), jnp.sin(angles))


def rotate(tensor, cosine, sine_vals):
    half_rot = cosine.shape[-1]
    front_part = tensor[..., :half_rot]
    back_part = tensor[..., half_rot : 2 * half_rot]
    rest_part = tensor[..., 2 * half_rot :]
    cosine_rows = cosine[:, None, :]
    sine_rows = sine_vals[:, None, :]
    return jnp.concatenate(
        [
            front_part * cosine_rows - back_part * sine_rows,
            back_part * cosine_rows + front_part * sine_rows,
            rest_part,
        ],
        axis=-1,
    )


def gelu_tanh(values_in):
    return jax.nn.gelu(values_in, approximate=True)


def local(
    tokens,
    cotangent,
    prefix_len,
    group_order,
    ln_gain,
    ln_bias,
    query_weight,
    query_bias,
    key_weight,
    key_bias,
    value_weight,
    value_bias,
    out_weight,
    out_bias,
    up_weight,
    up_bias,
    down_weight,
    down_bias,
):
    seq_count, local_rows, model_width = tokens.shape
    token_count = seq_count * local_rows
    inner_width = query_weight.shape[1]
    local_heads = inner_width // HD
    hidden_units = up_weight.shape[1]
    group_len = SEQ_LEN // group_order.shape[0]
    score_scale = HD ** (-0.5)
    own_place = positions(group_order, lax.axis_index("ctx") * local_rows, local_rows, group_len)
    key_place = positions(group_order, 0, SEQ_LEN, group_len)
    cosine, sine_vals = rotary_tables(own_place)
    allowed = (key_place[None, None, None, :] <= own_place[None, None, :, None]) | (
        key_place[None, None, None, :] < prefix_len[:, None, None, None]
    )
    gathered = (
        lax.all_gather(query_weight, "fsdp", axis=0, tiled=True),
        lax.all_gather(key_weight, "fsdp", axis=0, tiled=True),
        lax.all_gather(value_weight, "fsdp", axis=0, tiled=True),
        lax.all_gather(out_weight, "fsdp", axis=0, tiled=True),
        lax.all_gather(up_weight, "fsdp", axis=0, tiled=True),
        lax.all_gather(down_weight, "fsdp", axis=0, tiled=True),
    )
    w_query, w_key, w_value, w_out, w_up, w_down = gathered
    inputs = tokens.reshape(token_count, model_width).astype(jnp.float32)
    centre = jnp.mean(inputs, axis=-1, keepdims=True)
    centred = inputs - centre
    inv_std = lax.rsqrt(jnp.mean(centred * centred, axis=-1, keepdims=True) + norm_eps)
    normed = centred * inv_std
    norm_gain = ln_gain.astype(jnp.float32)
    hidden = (normed * norm_gain + ln_bias.astype(jnp.float32)).astype(jnp.bfloat16)

    def project(weight, bias_vec):
        return jnp.dot(hidden, weight, preferred_element_type=jnp.float32) + bias_vec.astype(
            jnp.float32
        )

    query_rot = rotate(
        project(w_query, query_bias).reshape(seq_count, local_rows, local_heads, HD),
        cosine,
        sine_vals,
    ).astype(jnp.bfloat16)
    key_rot = (
        rotate(
            project(w_key, key_bias).reshape(seq_count, local_rows, local_heads, HD),
            cosine,
            sine_vals,
        )
        .astype(jnp.bfloat16)
        .reshape(seq_count, local_rows, inner_width)
    )
    value_rows = (
        project(w_value, value_bias)
        .astype(jnp.bfloat16)
        .reshape(seq_count, local_rows, inner_width)
    )
    keys_all, values_all = (
        lax.all_gather(key_rot, "ctx", axis=1, tiled=True),
        lax.all_gather(value_rows, "ctx", axis=1, tiled=True),
    )

    def scores_for(key_block):
        key_heads = key_block.reshape(seq_count, key_block.shape[1], local_heads, HD)
        raw_scores = (
            jnp.einsum("bqhd,bkhd->bhqk", query_rot, key_heads, preferred_element_type=jnp.float32)
            * score_scale
        )
        return jnp.where(allowed, raw_scores, masked_fill)

    masked = scores_for(keys_all)
    row_max = jnp.max(masked, axis=-1, keepdims=True)
    exponent = jnp.exp(masked - row_max)
    row_total = jnp.sum(exponent, axis=-1, keepdims=True)
    attn_probs = (exponent / row_total).astype(jnp.bfloat16)
    log_total = row_max + jnp.log(row_total)
    value_heads = values_all.reshape(seq_count, values_all.shape[1], local_heads, HD)
    context = jnp.einsum(
        "bhqk,bkhd->bqhd", attn_probs, value_heads, preferred_element_type=jnp.float32
    )
    context = context.reshape(token_count, inner_width).astype(jnp.bfloat16)
    up_proj = project(w_up, up_bias)
    activated = gelu_tanh(up_proj).astype(jnp.bfloat16)
    partial_out = jnp.dot(context, w_out.T, preferred_element_type=jnp.float32) + jnp.dot(
        activated, w_down.T, preferred_element_type=jnp.float32
    )
    branches = lax.psum(partial_out, "tp")
    output = inputs + branches + out_bias.astype(jnp.float32) + down_bias.astype(jnp.float32)
    output = output.astype(jnp.bfloat16).reshape(seq_count, local_rows, model_width)
    back_query, back_key, back_value, back_out, back_up, back_down = (
        lax.all_gather(query_weight, "fsdp", axis=0, tiled=True),
        lax.all_gather(key_weight, "fsdp", axis=0, tiled=True),
        lax.all_gather(value_weight, "fsdp", axis=0, tiled=True),
        lax.all_gather(out_weight, "fsdp", axis=0, tiled=True),
        lax.all_gather(up_weight, "fsdp", axis=0, tiled=True),
        lax.all_gather(down_weight, "fsdp", axis=0, tiled=True),
    )
    keys_back, values_back = (
        lax.all_gather(key_rot, "ctx", axis=1, tiled=True),
        lax.all_gather(value_rows, "ctx", axis=1, tiled=True),
    )
    grad_out = cotangent.reshape(token_count, model_width)
    grad_context = jnp.dot(grad_out, back_out, preferred_element_type=jnp.float32).astype(
        jnp.bfloat16
    )
    grad_heads = grad_context.reshape(seq_count, local_rows, local_heads, HD)
    key_heads_back = keys_back.reshape(seq_count, keys_back.shape[1], local_heads, HD)
    value_heads_back = values_back.reshape(seq_count, values_back.shape[1], local_heads, HD)
    probs_back = jnp.exp(scores_for(keys_back) - log_total)
    grad_probs = jnp.einsum(
        "bqhd,bkhd->bhqk", grad_heads, value_heads_back, preferred_element_type=jnp.float32
    )
    row_delta = jnp.sum(probs_back * grad_probs, axis=-1, keepdims=True)
    grad_scores = (probs_back * (grad_probs - row_delta)).astype(jnp.bfloat16)
    probs_low = probs_back.astype(jnp.bfloat16)
    grad_query_rot = (
        jnp.einsum(
            "bhqk,bkhd->bqhd", grad_scores, key_heads_back, preferred_element_type=jnp.float32
        )
        * score_scale
    )
    row_count = local_rows * lax.axis_size("ctx")
    grad_key_part = (
        jnp.einsum("bhqk,bqhd->kbhd", grad_scores, query_rot, preferred_element_type=jnp.float32)
        * score_scale
    )
    grad_value_part = jnp.einsum(
        "bhqk,bqhd->kbhd", probs_low, grad_heads, preferred_element_type=jnp.float32
    )
    key_grads = lax.psum_scatter(
        jnp.concatenate(
            [
                grad_key_part.reshape(row_count, seq_count, inner_width),
                grad_value_part.reshape(row_count, seq_count, inner_width),
            ],
            axis=2,
        ),
        "ctx",
        scatter_dimension=0,
        tiled=True,
    )
    key_grads = jnp.transpose(key_grads, (1, 0, 2))
    key_grad_rot = key_grads[:, :, :inner_width].reshape(seq_count, local_rows, local_heads, HD)
    grad_value = (
        key_grads[:, :, inner_width:].astype(jnp.bfloat16).reshape(token_count, inner_width)
    )
    grad_query = (
        rotate(grad_query_rot, cosine, -sine_vals)
        .astype(jnp.bfloat16)
        .reshape(token_count, inner_width)
    )
    grad_key = (
        rotate(key_grad_rot, cosine, -sine_vals)
        .astype(jnp.bfloat16)
        .reshape(token_count, inner_width)
    )
    grad_activated = jnp.dot(grad_out, back_down, preferred_element_type=jnp.float32)
    gelu_pull = jax.vjp(gelu_tanh, up_proj)[1]
    grad_up = gelu_pull(grad_activated)[0].astype(jnp.bfloat16)
    partial_hidden = (
        jnp.dot(grad_query, back_query.T, preferred_element_type=jnp.float32)
        + jnp.dot(grad_key, back_key.T, preferred_element_type=jnp.float32)
        + jnp.dot(grad_value, back_value.T, preferred_element_type=jnp.float32)
        + jnp.dot(grad_up, back_up.T, preferred_element_type=jnp.float32)
    )
    grad_hidden = lax.psum(partial_hidden, "tp")
    grad_scaled = grad_hidden * norm_gain
    grad_normed = inv_std * (
        grad_scaled
        - jnp.mean(grad_scaled, axis=-1, keepdims=True)
        - normed * jnp.mean(grad_scaled * normed, axis=-1, keepdims=True)
    )
    grad_float = grad_out.astype(jnp.float32)
    input_grad = (
        (grad_float + grad_normed).astype(jnp.bfloat16).reshape(seq_count, local_rows, model_width)
    )
    small_terms = (
        jnp.sum(grad_hidden * normed, axis=0),
        jnp.sum(grad_hidden, axis=0),
        jnp.sum(grad_query, axis=0, dtype=jnp.float32),
        jnp.sum(grad_key, axis=0, dtype=jnp.float32),
        jnp.sum(grad_value, axis=0, dtype=jnp.float32),
        jnp.sum(grad_up, axis=0, dtype=jnp.float32),
        jnp.sum(grad_float, axis=0),
    )
    gain_grad, shift_grad, qbias_grad, kbias_grad, vbias_grad, ubias_grad, obias_grad = lax.psum(
        (
            small_terms[0],
            small_terms[1],
            small_terms[2],
            small_terms[3],
            small_terms[4],
            small_terms[5],
            small_terms[6],
        ),
        ("fsdp", "ctx"),
    )
    grads_in = jnp.concatenate([grad_query, grad_key, grad_value, grad_up], axis=1)
    acts_out = jnp.concatenate([context, activated], axis=1)
    left_part = jnp.einsum("tc,tn->cn", hidden, grads_in, preferred_element_type=jnp.float32)
    right_part = jnp.einsum("tc,tn->cn", grad_out, acts_out, preferred_element_type=jnp.float32)
    scattered = lax.psum_scatter(
        jnp.concatenate([left_part, right_part], axis=1), "fsdp", scatter_dimension=0, tiled=True
    )
    weight_grads = lax.psum(scattered, "ctx")
    edge_two = 2 * inner_width
    edge_three = 3 * inner_width
    edge_four = edge_three + hidden_units
    edge_five = edge_four + inner_width
    return (
        output,
        input_grad,
        gain_grad,
        shift_grad,
        weight_grads[:, :inner_width],
        qbias_grad,
        weight_grads[:, inner_width:edge_two],
        kbias_grad,
        weight_grads[:, edge_two:edge_three],
        vbias_grad,
        weight_grads[:, edge_four:edge_five],
        weight_grads[:, edge_three:edge_four],
        ubias_grad,
        weight_grads[:, edge_five:],
        obias_grad,
    )


def solution(mesh):
    return jax.shard_map(
        local,
        mesh=mesh,
        in_specs=(
            P("fsdp", "ctx", None),
            P("fsdp", "ctx", None),
            P("fsdp"),
            P(),
            P(),
            P(),
            P("fsdp", "tp"),
            P("tp"),
            P("fsdp", "tp"),
            P("tp"),
            P("fsdp", "tp"),
            P("tp"),
            P("fsdp", "tp"),
            P(),
            P("fsdp", "tp"),
            P("tp"),
            P("fsdp", "tp"),
            P(),
        ),
        out_specs=(
            P("fsdp", "ctx", None),
            P("fsdp", "ctx", None),
            P(),
            P(),
            P("fsdp", "tp"),
            P("tp"),
            P("fsdp", "tp"),
            P("tp"),
            P("fsdp", "tp"),
            P("tp"),
            P("fsdp", "tp"),
            P("fsdp", "tp"),
            P("tp"),
            P("fsdp", "tp"),
            P(),
        ),
        check_vma=False,
    )
```

profile of v0, /device:TPU:0, one launch (start us, length us, event | category | flops | bytes accessed | tf_op | source)
XLA Modules:
  0.0 2836.2 jit_solution(8669938643243681293)
XLA Ops:
  11.8 2.2 fusion.32
  14.0 51.3 %all-gather.9.cloned.1.call-done = bf16[2048,1024]{1,0:T(8,128)(2,1)} async-done(((bf16[512,1024]{1,0:T(8,128)(2,1)}), bf16[2048,1024]{1,0:T(8,128)(2,1)}) %all-gather.9.cloned.1.call-update) | async-done | bytes 4194320 | tf_op jit(solution)/shard_map/all_gather | solution.py:86
  65.3 6.1 add_convert_fusion
  72.7 47.3 %all-gather.15.cloned.1.call-done = bf16[2048,1024]{1,0:T(8,128)(2,1)} async-done(((bf16[512,1024]{1,0:T(8,128)(2,1)}), bf16[2048,1024]{1,0:T(8,128)(2,1)}) %all-gather.15.cloned.1.call-update) | async-done | bytes 4194320 | tf_op jit(solution)/shard_map/all_gather | solution.py:85
  119.9 5.8 convolution_add_fusion.1
  125.8 2.9 copy.73
  128.6 3.7 reshape.388
  132.3 2.5 slice.114
  134.8 39.8 %all-gather.13.cloned.1.call-done = bf16[2048,1024]{1,0:T(8,128)(2,1)} async-done(((bf16[512,1024]{1,0:T(8,128)(2,1)}), bf16[2048,1024]{1,0:T(8,128)(2,1)}) %all-gather.13.cloned.1.call-update) | async-done | bytes 4194320 | tf_op jit(solution)/shard_map/all_gather | solution.py:84
  174.5 5.8 convolution_add_fusion.2
  180.3 4.5 reshape.399
  184.9 8.3 fusion.57
  193.2 3.6 copy.98
  196.8 3.5 copy.97
  202.3 1.5 pad_maximum_fusion.3
  207.9 2.8 slice.85
  210.7 18.2 all-gather.19.cloned.1.call-done
  228.9 5.2 convolution_convert_fusion
  234.1 2.7 reshape.400
  236.8 2.9 copy.81
  239.7 2.4 copy.99
  242.1 69.7 %all-gather.11.cloned.1.call-done = bf16[2,1024,1024]{2,1,0:T(8,128)(2,1)} async-done(((bf16[2,256,1024]{2,1,0:T(8,128)(2,1)}), bf16[2,1024,1024]{2,1,0:T(8,128)(2,1)}) %all-gather.11.cloned.1.call-update) | async-done | bytes 4194320 | tf_op jit(solution)/shard_map/all_gather | solution.py:126
  311.7 6.2 copy.68
  318.0 74.9 %all-gather.17.cloned.1.call-done = bf16[2,1024,1024]{1,2,0:T(8,128)(2,1)} async-done(((bf16[2,256,1024]{1,2,0:T(8,128)(2,1)}), bf16[2,1024,1024]{1,2,0:T(8,128)(2,1)}) %all-gather.17.cloned.1.call-update) | async-done | bytes 4194320 | tf_op jit(solution)/shard_map/all_gather | solution.py:125
  392.9 20.1 fusion.59
  412.9 14.6 fusion
  427.5 22.3 multiply_reduce_fusion
  449.8 29.6 %multiply_convert_fusion = bf16[2,16,256,1024]{3,2,1,0:T(8,128)(2,1)} fusion(f32[2,16,256,1024]{3,2,1,0:T(8,128)} %get-tuple-element.72, f32[2,16,256,1024]{3,2,1,0:T(8,128)} %get-tuple-element.70, f32[2,16,256]{2,1,0:T(8,128)S(1)} %get-tuple-element.71, f32[2,16,256]{2,1,0:T(8,128)S(1)} %log_add_fusion), kind=kLoop, calls=%fused_computation.1 | loop fusion | flops 33554432 | bytes 83951616 | tf_op jit(solution)/shard_map/convert_element_type | solution.py:180
  479.4 12.2 broadcast_multiply_fusion
  491.6 17.0 fusion.2
  508.6 11.9 pad_maximum_fusion.1
  521.2 15.1 fusion.43
  538.6 1.3 copy.88
  539.9 13.7 multiply_bitcast_fusion
  553.6 1.3 slice.91
  554.9 14.4 fusion.61
  569.3 140.3 %all-gather.23.cloned.1.call-done = bf16[2048,4096]{1,0:T(8,128)(2,1)} async-done(((bf16[512,4096]{1,0:T(8,128)(2,1)}), bf16[2048,4096]{1,0:T(8,128)(2,1)}) %all-gather.23.cloned.1.call-update) | async-done | bytes 16777232 | tf_op jit(solution)/shard_map/all_gather | solution.py:89
  709.6 22.4 convert_reduce_fusion
  732.1 22.1 convolution_bitcast_fusion
  754.2 238.2 %reduce-scatter.3.cloned.1.call-done = f32[256,2,2048]{0,2,1:T(8,128)} async-done(((f32[1024,2,2048]{0,2,1:T(8,128)}), f32[256,2,2048]{0,2,1:T(8,128)}) %reduce-scatter.3.cloned.1.call-update) | async-done | bytes 4194320 | tf_op jit(solution)/shard_map/reduce_scatter | solution.py:196
  992.3 4.0 convert_reduce_fusion.3
  996.8 1.9 convert_reduce_fusion.4
  1000.0 1.3 copy.87
  1001.3 2.3 copy.82
  1003.6 1.2 copy.103
  1004.9 2.3 copy.86
  1007.1 1.5 copy.85
  1008.6 26.3 fusion.13
  1034.9 65.5 %pad_maximum_fusion = f32[2048,12288]{1,0:T(8,128)} fusion(f32[2048,5120]{1,0:T(8,128)} %convolution_bitcast_fusion, f32[2048,7168]{1,0:T(8,128)} %fusion.13), kind=kLoop, calls=%fused_computation | loop fusion | flops 25165824 | bytes 201326592 | tf_op jit(solution)/shard_map/concatenate | solution.py:269
  1101.7 6.7 fusion.60
  1108.4 16.2 convolution_add_fusion
  1124.6 4.4 fusion.63
  1129.0 4.4 fusion.62
  1133.4 4.4 fusion.64
  1137.8 18.3 add_add_fusion
  1156.2 773.7 %reduce-scatter.5.cloned.1.call-done = f32[512,12288]{1,0:T(8,128)} async-done(((f32[2048,12288]{1,0:T(8,128)}), f32[512,12288]{1,0:T(8,128)}) %reduce-scatter.5.cloned.1.call-update) | async-done | bytes 25165840 | tf_op jit(solution)/shard_map/reduce_scatter | solution.py:268
  1930.6 2.0 convert_reduce_fusion.2
  1932.8 39.2 %all-reduce.7.cloned.1.call-done = (f32[512,2048]{1,0:T(8,128)}, f32[512,2048]{1,0:T(8,128)}) async-done(((f32[512,2048]{1,0:T(8,128)}, f32[512,2048]{1,0:T(8,128)}), (f32[512,2048]{1,0:T(8,128)}, f32[512,2048]{1,0:T(8,128)})) %all-reduce.7.cloned.1.call-update) | async-done | bytes 8388624 | tf_op jit(solution)/shard_map/psum | solution.py:153
  1972.0 3.6 fusion.38
  1975.7 82.3 %all-reduce = (f32[2048]{0:T(1024)}, f32[2048]{0:T(1024)}, f32[1024]{0:T(1024)}, f32[1024]{0:T(1024)}, f32[1024]{0:T(1024)}, /*index=5*/f32[4096]{0:T(1024)}, f32[2048]{0:T(1024)}) all-reduce(f32[2048]{0:T(1024)S(1)} %get-tuple-element.15, f32[2048]{0:T(1024)S(1)} %get-tuple-element.18, ...), channel_id=1, replica_groups=mesh['fsdp'=4,'ctx'=4,'tp'=2] {'fsdp','ctx'}, use_global_device_ids=true, to_apply=%region_13.14 | all-reduce | flops 13312 | bytes 106496 | tf_op jit(solution)/shard_map/psum | solution.py:252
  2058.0 6.8 fusion.37
  2064.8 745.8 %all-reduce.5.cloned.1.call-done = f32[512,12288]{1,0:T(8,128)} async-done(((f32[512,12288]{1,0:T(8,128)}), f32[512,12288]{1,0:T(8,128)}) %all-reduce.5.cloned.1.call-update) | async-done | bytes 25165840 | tf_op jit(solution)/shard_map/psum | solution.py:271
  2810.6 7.5 fusion.56
  2818.1 11.1 fusion.55
  (150 shorter events, 18.5 us)
Async XLA Ops:
  7.2 2.9 copy-start
  7.2 4.0 copy-start.34
  7.2 4.0 copy-start.30
  7.2 4.0 copy-start.31
  7.2 58.1 %all-gather.9.cloned.1.call-start = ((), (), s32[]{:S(2)}) async-start(), calls=%async_computation.2 | async-start | bytes 5242880 | tf_op jit(solution)/shard_map/all_gather | solution.py:86
  8.0 112.0 %all-gather.15.cloned.1.call-start = ((), (), s32[]{:S(2)}) async-start(), calls=%async_computation.5 | async-start | bytes 5242880 | tf_op jit(solution)/shard_map/all_gather | solution.py:85
  8.7 165.8 %all-gather.13.cloned.1.call-start = ((), (), s32[]{:S(2)}) async-start(), calls=%async_computation.4 | async-start | bytes 5242880 | tf_op jit(solution)/shard_map/all_gather | solution.py:84
  9.4 219.5 %all-gather.19.cloned.1.call-start = ((), (), s32[]{:S(2)}) async-start(), calls=%async_computation.7 | async-start | bytes 5242880 | tf_op jit(solution)/shard_map/all_gather | solution.py:87
  10.0 301.7 %all-gather.11.cloned.1.call-start = ((), (), s32[]{:S(2)}) async-start(), calls=%async_computation.3 | async-start | bytes 5242880 | tf_op jit(solution)/shard_map/all_gather | solution.py:126
  10.4 0.8 copy-start.21
  11.2 0.6 copy-start.23
  11.2 0.6 copy-start.18
  14.0 57.7 %copy-start.35 = (bf16[1024]{0:T(1024)(128)(2,1)S(1)}, bf16[1024]{0:T(1024)(128)(2,1)}, u32[]{:S(2)}) copy-start(bf16[1024]{0:T(1024)(128)(2,1)} %param.25) | copy-start | bytes 6148
  14.0 57.8 %copy-start.36 = (bf16[1024]{0:T(1024)(128)(2,1)S(1)}, bf16[1024]{0:T(1024)(128)(2,1)}, u32[]{:S(2)}) copy-start(bf16[1024]{0:T(1024)(128)(2,1)} %param.27) | copy-start | bytes 6148
  14.0 57.8 %copy-start.37 = (s32[8]{0:T(128)S(1)}, s32[8]{0:T(128)}, u32[]{:S(2)}) copy-start(s32[8]{0:T(128)} %param.21) | copy-start | bytes 100
  14.0 105.9 %copy-start.3 = (bf16[512,2048]{1,0:T(8,128)(2,1)S(1)}, bf16[512,2048]{1,0:T(8,128)(2,1)}, u32[]{:S(2)}) copy-start(bf16[512,2048]{1,0:T(8,128)(2,1)} %fusion.32) | copy-start | bytes 6291460
  71.5 321.4 %all-gather.17.cloned.1.call-start = ((), (), s32[]{:S(2)}) async-start(), calls=%async_computation.6 | async-start | bytes 5242880 | tf_op jit(solution)/shard_map/all_gather | solution.py:125
  72.7 128.0 %copy-start.16 = (f32[256,16]{0,1:T(8,128)}, f32[256,16]{0,1:T(8,128)S(1)}, u32[]{:S(2)}) copy-start(f32[256,16]{0,1:T(8,128)S(1)} %get-tuple-element.68) | copy-start | bytes 49156
  193.2 7.1 copy-start.5
  200.3 2.0 copy-start.15
  204.9 1.7 copy-start.38
  204.9 350.0 %all-gather.21.cloned.1.call-start = ((), (), s32[]{:S(2)}) async-start(), calls=%async_computation.8 | async-start | bytes 20971520 | tf_op jit(solution)/shard_map/all_gather | solution.py:88
  205.7 503.9 %all-gather.23.cloned.1.call-start = ((), (), s32[]{:S(2)}) async-start(), calls=%async_computation.9 | async-start | bytes 20971520 | tf_op jit(solution)/shard_map/all_gather | solution.py:89
  206.4 785.9 %reduce-scatter.3.cloned.1.call-start = ((), (), s32[]{:S(2)}) async-start(), calls=%async_computation.10 | async-start | bytes 20971520 | tf_op jit(solution)/shard_map/reduce_scatter | solution.py:196
  242.1 150.8 %copy-start.7 = (bf16[2,256,16,32]{1,3,2,0:T(8,128)(2,1)S(1)}, bf16[2,256,16,32]{1,3,2,0:T(8,128)(2,1)}, u32[]{:S(2)}) copy-start(bf16[2,256,16,32]{1,3,2,0:T(8,128)(2,1)} %copy.99) | copy-start | bytes 1572868
  242.1 150.8 %copy-start.8 = (pred[2,256,1024]{2,1,0:T(8,128)(4,1)S(1)}, pred[2,256,1024]{2,1,0:T(8,128)(4,1)}, u32[]{:S(2)}) copy-start(pred[2,256,1024]{2,1,0:T(8,128)(4,1)} %broadcast_or_fusion) | copy-start | bytes 1572868
  242.1 150.8 %copy-start.14 = (bf16[2,256,16,16]{1,3,2,0:T(8,128)(2,1)S(1)}, bf16[2,256,16,16]{1,3,2,0:T(8,128)(2,1)}, u32[]{:S(2)}) copy-start(bf16[2,256,16,16]{1,3,2,0:T(8,128)(2,1)} %get-tuple-element.57) | copy-start | bytes 786436
  412.9 14.6 copy-start.2
  520.5 0.7 copy-start.29
  520.5 1409.4 %reduce-scatter.5.cloned.1.call-start = ((), (), s32[]{:S(2)}) async-start(), calls=%async_computation.11 | async-start | bytes 125829120 | tf_op jit(solution)/shard_map/reduce_scatter | solution.py:268
  537.6 1.0 copy-start.9
  539.9 15.0 copy-start.4
  754.1 242.3 %copy-start.17 = (f32[256,16]{0,1:T(8,128)S(1)}, f32[256,16]{0,1:T(8,128)}, u32[]{:S(2)}) copy-start(f32[256,16]{0,1:T(8,128)} %copy-done.16) | copy-start | bytes 49156
  754.1 242.3 %copy-start.20 = (f32[256,16]{0,1:T(8,128)S(1)}, f32[256,16]{0,1:T(8,128)}, u32[]{:S(2)}) copy-start(f32[256,16]{0,1:T(8,128)} %get-tuple-element.66) | copy-start | bytes 49156
  992.3 4.1 copy-start.6
  1000.0 7.1 copy-start.11
  1100.5 1.2 copy-start.10
  1100.5 871.5 %all-reduce.7.cloned.1.call-start = ((), (), s32[]{:S(2)}) async-start(), calls=%async_computation.13 | async-start | bytes 16777216 | tf_op jit(solution)/shard_map/psum | solution.py:153
  1108.4 16.2 copy-start.12
  1108.4 16.2 copy-start.40
  1124.6 4.4 copy-start.13
  1124.6 4.4 copy-start.41
  1129.0 4.4 copy-start.39
  1156.2 1654.4 %all-reduce.5.cloned.1.call-start = ((), (), s32[]{:S(2)}) async-start(), calls=%async_computation.12 | async-start | bytes 50331648 | tf_op jit(solution)/shard_map/psum | solution.py:271
  1929.9 0.7 copy-start.32
  1929.9 0.7 copy-start.33
  1929.9 2.7 copy-start.26
  1929.9 2.8 copy-start.25
  1929.9 42.1 %copy-start.1 = (bf16[2,256,2048]{2,1,0:T(8,128)(2,1)S(1)}, bf16[2,256,2048]{2,1,0:T(8,128)(2,1)}, u32[]{:S(2)}) copy-start(bf16[2,256,2048]{2,1,0:T(8,128)(2,1)} %param.18) | copy-start | bytes 6291460
  1929.9 42.1 %copy-start.19 = (f32[2048]{0:T(1024)S(1)}, f32[2048]{0:T(1024)}, u32[]{:S(2)}) copy-start(f32[2048]{0:T(1024)} %copy-done.18) | copy-start | bytes 24580
  1929.9 42.1 %copy-start.22 = (f32[1,2,2,128]{3,1,2,0:T(2,128)S(1)}, f32[1,2,2,128]{3,1,2,0:T(2,128)}, u32[]{:S(2)}) copy-start(f32[1,2,2,128]{3,1,2,0:T(2,128)} %copy-done.21) | copy-start | bytes 6148
  1929.9 42.0 %copy-start.24 = (f32[1,2,2,128]{3,1,2,0:T(2,128)S(1)}, f32[1,2,2,128]{3,1,2,0:T(2,128)}, u32[]{:S(2)}) copy-start(f32[1,2,2,128]{3,1,2,0:T(2,128)} %copy-done.23) | copy-start | bytes 6148
  1930.6 45.0 %copy-start.27 = (f32[4096]{0:T(1024)S(1)}, f32[4096]{0:T(1024)}, u32[]{:S(2)}) copy-start(f32[4096]{0:T(1024)} %get-tuple-element.28) | copy-start | bytes 49156
  1930.6 45.0 %copy-start.28 = (f32[1024]{0:T(1024)S(1)}, f32[1024]{0:T(1024)}, u32[]{:S(2)}) copy-start(f32[1024]{0:T(1024)} %get-tuple-element.30) | copy-start | bytes 12292
Sparse Core Ops, SparseCore 0:
  9.9 55.3 all-gather.8
  67.2 52.6 all-gather.14
  121.8 52.6 all-gather.12
  176.2 52.6 all-gather.18
  230.9 80.7 all-gather.10
  313.7 79.0 all-gather.16
  394.7 155.5 all-gather.20
  552.2 157.4 all-gather.22
  712.0 280.2 reduce-scatter.2
  1100.6 829.2 reduce-scatter.4
  1933.0 38.8 all-reduce.6
  1974.3 836.1 all-reduce.4
where the time goes:
time: 2840 us
  waiting for transfers between devices  2240 us (79%)
  matrix products  263 us (9%)
  other arithmetic  148 us (5%)
  local copies, waits for them, and re-layouts  84.7 us (3%)
  blocking collectives  82.3 us (3%)
    reduce_scatter x1, waiting for transfers between devices, local(): lax.psum_scatter(jnp.concatenate([left_part, right_part], axis=1), 'fsdp'...  774 us
    psum x1, waiting for transfers between devices, local(): weight_grads = lax.psum(scattered, 'ctx')  746 us
    reduce_scatter x1, waiting for transfers between devices, local(): lax.psum_scatter(jnp.concatenate([grad_key_part.reshape(row_count, seq_co...  238 us
    all_gather x1, waiting for transfers between devices, local(): lax.all_gather(down_weight, 'fsdp', axis=0, tiled=True)  140 us
    psum x1, blocking collectives, local(): lax.psum((small_terms[0], small_terms[1], small_terms[2], small_terms[3],...  82.3 us
    all_gather x1, waiting for transfers between devices, local(): lax.all_gather(key_rot, 'ctx', axis=1, tiled=True)  74.9 us
    all_gather x1, waiting for transfers between devices, local(): lax.all_gather(value_rows, 'ctx', axis=1, tiled=True)  69.7 us
    concatenate x1, other arithmetic, local(): jnp.concatenate([left_part, right_part], axis=1)  65.5 us
  transfers between devices with their start and end apart: 12, of which 11 were waited for; matrix products, arithmetic and copies ran while one was open for 13% of the time, Pallas kernels for 0%

commit v1 on v0

--- a/solution.py
+++ b/solution.py
@@ -268,7 +268,7 @@
     scattered = lax.psum_scatter(
         jnp.concatenate([left_part, right_part], axis=1), "fsdp", scatter_dimension=0, tiled=True
     )
-    weight_grads = lax.psum(scattered, "ctx")
+    weight_grads = jnp.sum(lax.all_gather(scattered, "ctx"), axis=0)
     edge_two = 2 * inner_width
     edge_three = 3 * inner_width
     edge_four = edge_three + hidden_units

time: 2840 us -> 3710 us (1.31)
  waiting for transfers between devices: 2240 us -> 2840 us
  blocking collectives: 82.3 us -> 313 us
  other arithmetic: 148 us -> 189 us
    all_gather x0 -> x1, waiting for transfers between devices: none -> 1340 us  [local(): weight_grads = jnp.sum(lax.all_gather(scattered, 'ctx'), axis=0)]
    psum x1 -> x0, waiting for transfers between devices: 746 us -> none  [local(): weight_grads = lax.psum(scattered, 'ctx')]
    psum x1, blocking collectives: 82.3 us -> 313 us  [local(): lax.psum((small_terms[0], small_terms[1], small_terms[2], small_terms[3],...]
    reduce_sum x0 -> x1, other arithmetic: none -> 40.5 us  [local(): weight_grads = jnp.sum(lax.all_gather(scattered, 'ctx'), axis=0)]
  transfers between devices with their start and end apart: 12 -> 12, of which waited for: 11 -> 11; matrix products, arithmetic and copies ran while one was open for 13% -> 10% of each run, Pallas kernels for 0% -> 0%
where the time goes in v1:
time: 3710 us; the launch traced here: 3700 us
  waiting for transfers between devices  2840 us (77%)
  blocking collectives  313 us (8%)
  matrix products  263 us (7%)
  other arithmetic  189 us (5%)
  local copies, waits for them, and re-layouts  84.7 us (2%)
    all_gather x1, waiting for transfers between devices, local(): weight_grads = jnp.sum(lax.all_gather(scattered, 'ctx'), axis=0)  1340 us
    reduce_scatter x1, waiting for transfers between devices, local(): lax.psum_scatter(jnp.concatenate([left_part, right_part], axis=1), 'fsdp'...  774 us
    psum x1, blocking collectives, local(): lax.psum((small_terms[0], small_terms[1], small_terms[2], small_terms[3],...  313 us
    reduce_scatter x1, waiting for transfers between devices, local(): lax.psum_scatter(jnp.concatenate([grad_key_part.reshape(row_count, seq_co...  238 us
    all_gather x1, waiting for transfers between devices, local(): lax.all_gather(down_weight, 'fsdp', axis=0, tiled=True)  140 us
    all_gather x1, waiting for transfers between devices, local(): lax.all_gather(key_rot, 'ctx', axis=1, tiled=True)  74.9 us
  transfers between devices with their start and end apart: 12, of which 11 were waited for; matrix products, arithmetic and copies ran while one was open for 10% of the time, Pallas kernels for 0%

profile of v1, /device:TPU:0, one launch (start us, length us, event | category | flops | bytes accessed | tf_op | source)
XLA Modules:
  0.0 3701.9 jit_solution(15606240173004738463)
XLA Ops:
  11.8 2.2 fusion.32
  14.0 51.3 %all-gather.11.cloned.1.call-done = bf16[2048,1024]{1,0:T(8,128)(2,1)} async-done(((bf16[512,1024]{1,0:T(8,128)(2,1)}), bf16[2048,1024]{1,0:T(8,128)(2,1)}) %all-gather.11.cloned.1.call-update) | async-done | bytes 4194320 | tf_op jit(solution)/shard_map/all_gather | solution.py:86
  65.3 6.1 add_convert_fusion
  72.7 47.2 %all-gather.17.cloned.1.call-done = bf16[2048,1024]{1,0:T(8,128)(2,1)} async-done(((bf16[512,1024]{1,0:T(8,128)(2,1)}), bf16[2048,1024]{1,0:T(8,128)(2,1)}) %all-gather.17.cloned.1.call-update) | async-done | bytes 4194320 | tf_op jit(solution)/shard_map/all_gather | solution.py:85
  119.9 5.8 convolution_add_fusion.1
  125.8 2.9 copy.73
  128.6 3.7 reshape.388
  132.3 2.5 slice.114
  134.8 39.8 %all-gather.15.cloned.1.call-done = bf16[2048,1024]{1,0:T(8,128)(2,1)} async-done(((bf16[512,1024]{1,0:T(8,128)(2,1)}), bf16[2048,1024]{1,0:T(8,128)(2,1)}) %all-gather.15.cloned.1.call-update) | async-done | bytes 4194320 | tf_op jit(solution)/shard_map/all_gather | solution.py:84
  174.5 5.8 convolution_add_fusion.2
  180.3 4.5 reshape.400
  184.9 8.3 fusion.57
  193.2 3.6 copy.98
  196.8 3.5 copy.97
  202.3 1.5 pad_maximum_fusion.3
  207.9 2.8 slice.85
  210.7 18.2 all-gather.21.cloned.1.call-done
  228.9 5.1 convolution_convert_fusion
  234.1 2.8 reshape.401
  236.9 2.9 copy.81
  239.8 2.4 copy.99
  242.1 69.6 %all-gather.13.cloned.1.call-done = bf16[2,1024,1024]{2,1,0:T(8,128)(2,1)} async-done(((bf16[2,256,1024]{2,1,0:T(8,128)(2,1)}), bf16[2,1024,1024]{2,1,0:T(8,128)(2,1)}) %all-gather.13.cloned.1.call-update) | async-done | bytes 4194320 | tf_op jit(solution)/shard_map/all_gather | solution.py:126
  311.7 6.2 copy.68
  318.0 74.9 %all-gather.19.cloned.1.call-done = bf16[2,1024,1024]{1,2,0:T(8,128)(2,1)} async-done(((bf16[2,256,1024]{1,2,0:T(8,128)(2,1)}), bf16[2,1024,1024]{1,2,0:T(8,128)(2,1)}) %all-gather.19.cloned.1.call-update) | async-done | bytes 4194320 | tf_op jit(solution)/shard_map/all_gather | solution.py:125
  392.9 20.1 fusion.59
  412.9 14.6 fusion
  427.5 22.3 multiply_reduce_fusion
  449.8 29.6 multiply_convert_fusion
  479.4 12.2 broadcast_multiply_fusion
  491.6 17.0 fusion.2
  508.6 11.9 pad_maximum_fusion.1
  521.2 15.1 fusion.43
  538.6 1.3 copy.88
  539.9 13.7 multiply_bitcast_fusion
  553.6 1.3 slice.91
  554.9 14.4 fusion.61
  569.3 140.3 %all-gather.25.cloned.1.call-done = bf16[2048,4096]{1,0:T(8,128)(2,1)} async-done(((bf16[512,4096]{1,0:T(8,128)(2,1)}), bf16[2048,4096]{1,0:T(8,128)(2,1)}) %all-gather.25.cloned.1.call-update) | async-done | bytes 16777232 | tf_op jit(solution)/shard_map/all_gather | solution.py:89
  709.6 22.4 convert_reduce_fusion
  732.1 22.1 convolution_bitcast_fusion
  754.2 238.2 %reduce-scatter.3.cloned.1.call-done = f32[256,2,2048]{0,2,1:T(8,128)} async-done(((f32[1024,2,2048]{0,2,1:T(8,128)}), f32[256,2,2048]{0,2,1:T(8,128)}) %reduce-scatter.3.cloned.1.call-update) | async-done | bytes 4194320 | tf_op jit(solution)/shard_map/reduce_scatter | solution.py:196
  992.3 4.0 convert_reduce_fusion.3
  996.8 1.9 convert_reduce_fusion.4
  1000.0 1.3 copy.87
  1001.3 2.3 copy.82
  1004.9 2.3 copy.86
  1007.1 1.5 copy.85
  1008.6 26.3 fusion.13
  1034.9 65.5 %pad_maximum_fusion = f32[2048,12288]{1,0:T(8,128)} fusion(f32[2048,5120]{1,0:T(8,128)} %convolution_bitcast_fusion, f32[2048,7168]{1,0:T(8,128)} %fusion.13), kind=kLoop, calls=%fused_computation | loop fusion | flops 25165824 | bytes 201326592 | tf_op jit(solution)/shard_map/concatenate | solution.py:269
  1101.7 6.7 fusion.60
  1108.4 16.2 convolution_add_fusion
  1124.6 4.4 fusion.63
  1129.0 4.4 fusion.62
  1133.4 4.4 fusion.64
  1137.8 18.3 add_add_fusion
  1156.2 773.7 %reduce-scatter.5.cloned.1.call-done = f32[512,12288]{1,0:T(8,128)} async-done(((f32[2048,12288]{1,0:T(8,128)}), f32[512,12288]{1,0:T(8,128)}) %reduce-scatter.5.cloned.1.call-update) | async-done | bytes 25165840 | tf_op jit(solution)/shard_map/reduce_scatter | solution.py:268
  1930.6 2.0 convert_reduce_fusion.2
  1932.8 39.2 %all-reduce.4.cloned.1.call-done = (f32[512,2048]{1,0:T(8,128)}, f32[512,2048]{1,0:T(8,128)}) async-done(((f32[512,2048]{1,0:T(8,128)}, f32[512,2048]{1,0:T(8,128)}), (f32[512,2048]{1,0:T(8,128)}, f32[512,2048]{1,0:T(8,128)})) %all-reduce.4.cloned.1.call-update) | async-done | bytes 8388624 | tf_op jit(solution)/shard_map/psum | solution.py:153
  1972.0 3.6 fusion.38
  1975.7 312.8 %all-reduce = (f32[2048]{0:T(1024)}, f32[2048]{0:T(1024)}, f32[1024]{0:T(1024)}, f32[1024]{0:T(1024)}, f32[1024]{0:T(1024)}, /*index=5*/f32[4096]{0:T(1024)}, f32[2048]{0:T(1024)}) all-reduce(f32[2048]{0:T(1024)S(1)} %get-tuple-element.15, f32[2048]{0:T(1024)S(1)} %get-tuple-element.18, ...), channel_id=1, replica_groups=mesh['fsdp'=4,'ctx'=4,'tp'=2] {'fsdp','ctx'}, use_global_device_ids=true, to_apply=%region_13.14 | all-reduce | flops 13312 | bytes 106496 | tf_op jit(solution)/shard_map/psum | solution.py:252
  2288.5 6.8 fusion.37
  2295.3 1340.2 %all-gather.27.cloned.1.call-done = f32[2048,12288]{1,0:T(8,128)} async-done(((f32[512,12288]{1,0:T(8,128)}), f32[2048,12288]{1,0:T(8,128)}) %all-gather.27.cloned.1.call-update) | async-done | bytes 100663312 | tf_op jit(solution)/shard_map/all_gather | solution.py:271
  3635.5 40.5 %reduce_sum.158 = f32[512,12288]{1,0:T(8,128)} reduce(f32[4,512,12288]{2,1,0:T(8,128)} %bitcast.18, f32[]{:T(128)} %constant.55.clone.1), dimensions={0}, to_apply=%region_17.18 | reduce | flops 18874368 | bytes 125829120 | tf_op jit(solution)/shard_map/reduce_sum | solution.py:271
  3676.0 7.5 fusion.56
  3683.5 11.1 fusion.55
  (151 shorter events, 19.7 us)
Async XLA Ops:
  7.2 2.9 copy-start
  7.2 4.0 copy-start.34
  7.2 4.0 copy-start.30
  7.2 4.0 copy-start.31
  7.2 58.1 %all-gather.11.cloned.1.call-start = ((), (), s32[]{:S(2)}) async-start(), calls=%async_computation.2 | async-start | bytes 5242880 | tf_op jit(solution)/shard_map/all_gather | solution.py:86
  8.0 112.0 %all-gather.17.cloned.1.call-start = ((), (), s32[]{:S(2)}) async-start(), calls=%async_computation.5 | async-start | bytes 5242880 | tf_op jit(solution)/shard_map/all_gather | solution.py:85
  8.7 165.8 %all-gather.15.cloned.1.call-start = ((), (), s32[]{:S(2)}) async-start(), calls=%async_computation.4 | async-start | bytes 5242880 | tf_op jit(solution)/shard_map/all_gather | solution.py:84
  9.4 219.5 %all-gather.21.cloned.1.call-start = ((), (), s32[]{:S(2)}) async-start(), calls=%async_computation.7 | async-start | bytes 5242880 | tf_op jit(solution)/shard_map/all_gather | solution.py:87
  10.0 301.7 %all-gather.13.cloned.1.call-start = ((), (), s32[]{:S(2)}) async-start(), calls=%async_computation.3 | async-start | bytes 5242880 | tf_op jit(solution)/shard_map/all_gather | solution.py:126
  10.4 0.8 copy-start.21
  11.2 0.6 copy-start.23
  11.2 0.6 copy-start.18
  14.0 57.8 %copy-start.35 = (bf16[1024]{0:T(1024)(128)(2,1)S(1)}, bf16[1024]{0:T(1024)(128)(2,1)}, u32[]{:S(2)}) copy-start(bf16[1024]{0:T(1024)(128)(2,1)} %param.25) | copy-start | bytes 6148
  14.0 57.8 %copy-start.36 = (bf16[1024]{0:T(1024)(128)(2,1)S(1)}, bf16[1024]{0:T(1024)(128)(2,1)}, u32[]{:S(2)}) copy-start(bf16[1024]{0:T(1024)(128)(2,1)} %param.27) | copy-start | bytes 6148
  14.0 57.9 %copy-start.37 = (s32[8]{0:T(128)S(1)}, s32[8]{0:T(128)}, u32[]{:S(2)}) copy-start(s32[8]{0:T(128)} %param.21) | copy-start | bytes 100
  14.0 105.9 %copy-start.3 = (bf16[512,2048]{1,0:T(8,128)(2,1)S(1)}, bf16[512,2048]{1,0:T(8,128)(2,1)}, u32[]{:S(2)}) copy-start(bf16[512,2048]{1,0:T(8,128)(2,1)} %fusion.32) | copy-start | bytes 6291460
  71.5 321.4 %all-gather.19.cloned.1.call-start = ((), (), s32[]{:S(2)}) async-start(), calls=%async_computation.6 | async-start | bytes 5242880 | tf_op jit(solution)/shard_map/all_gather | solution.py:125
  72.7 128.0 %copy-start.16 = (f32[256,16]{0,1:T(8,128)}, f32[256,16]{0,1:T(8,128)S(1)}, u32[]{:S(2)}) copy-start(f32[256,16]{0,1:T(8,128)S(1)} %get-tuple-element.68) | copy-start | bytes 49156
  193.2 7.1 copy-start.5
  200.3 2.0 copy-start.15
  204.9 1.7 copy-start.38
  204.9 350.0 %all-gather.23.cloned.1.call-start = ((), (), s32[]{:S(2)}) async-start(), calls=%async_computation.8 | async-start | bytes 20971520 | tf_op jit(solution)/shard_map/all_gather | solution.py:88
  205.7 503.9 %all-gather.25.cloned.1.call-start = ((), (), s32[]{:S(2)}) async-start(), calls=%async_computation.9 | async-start | bytes 20971520 | tf_op jit(solution)/shard_map/all_gather | solution.py:89
  206.4 785.9 %reduce-scatter.3.cloned.1.call-start = ((), (), s32[]{:S(2)}) async-start(), calls=%async_computation.10 | async-start | bytes 20971520 | tf_op jit(solution)/shard_map/reduce_scatter | solution.py:196
  242.1 150.7 %copy-start.7 = (bf16[2,256,16,32]{1,3,2,0:T(8,128)(2,1)S(1)}, bf16[2,256,16,32]{1,3,2,0:T(8,128)(2,1)}, u32[]{:S(2)}) copy-start(bf16[2,256,16,32]{1,3,2,0:T(8,128)(2,1)} %copy.99) | copy-start | bytes 1572868
  242.1 150.7 %copy-start.8 = (pred[2,256,1024]{2,1,0:T(8,128)(4,1)S(1)}, pred[2,256,1024]{2,1,0:T(8,128)(4,1)}, u32[]{:S(2)}) copy-start(pred[2,256,1024]{2,1,0:T(8,128)(4,1)} %broadcast_or_fusion) | copy-start | bytes 1572868
  242.1 150.7 %copy-start.14 = (bf16[2,256,16,16]{1,3,2,0:T(8,128)(2,1)S(1)}, bf16[2,256,16,16]{1,3,2,0:T(8,128)(2,1)}, u32[]{:S(2)}) copy-start(bf16[2,256,16,16]{1,3,2,0:T(8,128)(2,1)} %get-tuple-element.57) | copy-start | bytes 786436
  412.9 14.6 copy-start.2
  520.5 0.7 copy-start.29
  520.5 1409.4 %reduce-scatter.5.cloned.1.call-start = ((), (), s32[]{:S(2)}) async-start(), calls=%async_computation.11 | async-start | bytes 125829120 | tf_op jit(solution)/shard_map/reduce_scatter | solution.py:268
  537.6 1.0 copy-start.9
  539.9 15.0 copy-start.4
  754.1 242.3 %copy-start.17 = (f32[256,16]{0,1:T(8,128)S(1)}, f32[256,16]{0,1:T(8,128)}, u32[]{:S(2)}) copy-start(f32[256,16]{0,1:T(8,128)} %copy-done.16) | copy-start | bytes 49156
  754.1 242.3 %copy-start.20 = (f32[256,16]{0,1:T(8,128)S(1)}, f32[256,16]{0,1:T(8,128)}, u32[]{:S(2)}) copy-start(f32[256,16]{0,1:T(8,128)} %get-tuple-element.66) | copy-start | bytes 49156
  992.3 4.1 copy-start.6
  1000.0 7.1 copy-start.11
  1100.5 1.2 copy-start.10
  1100.5 871.5 %all-reduce.4.cloned.1.call-start = ((), (), s32[]{:S(2)}) async-start(), calls=%async_computation.13 | async-start | bytes 16777216 | tf_op jit(solution)/shard_map/psum | solution.py:153
  1108.4 16.2 copy-start.12
  1108.4 16.2 copy-start.40
  1124.6 4.4 copy-start.13
  1124.6 4.4 copy-start.41
  1129.0 4.4 copy-start.39
  1156.2 2479.4 %all-gather.27.cloned.1.call-start = ((), (), s32[]{:S(2)}) async-start(), calls=%async_computation.12 | async-start | bytes 125829120 | tf_op jit(solution)/shard_map/all_gather | solution.py:271
  1929.9 0.7 copy-start.32
  1929.9 0.7 copy-start.33
  1929.9 2.7 copy-start.26
  1929.9 2.8 copy-start.25
  1929.9 42.1 %copy-start.1 = (bf16[2,256,2048]{2,1,0:T(8,128)(2,1)S(1)}, bf16[2,256,2048]{2,1,0:T(8,128)(2,1)}, u32[]{:S(2)}) copy-start(bf16[2,256,2048]{2,1,0:T(8,128)(2,1)} %param.18) | copy-start | bytes 6291460
  1929.9 42.1 %copy-start.19 = (f32[2048]{0:T(1024)S(1)}, f32[2048]{0:T(1024)}, u32[]{:S(2)}) copy-start(f32[2048]{0:T(1024)} %copy-done.18) | copy-start | bytes 24580
  1929.9 42.1 %copy-start.22 = (f32[1,2,2,128]{3,1,2,0:T(2,128)S(1)}, f32[1,2,2,128]{3,1,2,0:T(2,128)}, u32[]{:S(2)}) copy-start(f32[1,2,2,128]{3,1,2,0:T(2,128)} %copy-done.21) | copy-start | bytes 6148
  1929.9 42.0 %copy-start.24 = (f32[1,2,2,128]{3,1,2,0:T(2,128)S(1)}, f32[1,2,2,128]{3,1,2,0:T(2,128)}, u32[]{:S(2)}) copy-start(f32[1,2,2,128]{3,1,2,0:T(2,128)} %copy-done.23) | copy-start | bytes 6148
  1930.6 45.0 %copy-start.27 = (f32[4096]{0:T(1024)S(1)}, f32[4096]{0:T(1024)}, u32[]{:S(2)}) copy-start(f32[4096]{0:T(1024)} %get-tuple-element.28) | copy-start | bytes 49156
  1930.6 45.0 %copy-start.28 = (f32[1024]{0:T(1024)S(1)}, f32[1024]{0:T(1024)}, u32[]{:S(2)}) copy-start(f32[1024]{0:T(1024)} %get-tuple-element.30) | copy-start | bytes 12292
Sparse Core Ops, SparseCore 0:
  9.9 55.3 all-gather.10
  67.2 52.6 all-gather.16
  121.8 52.6 all-gather.14
  176.2 52.6 all-gather.20
  230.9 80.7 all-gather.12
  313.7 79.0 all-gather.18
  394.7 155.5 all-gather.22
  552.2 157.4 all-gather.24
  712.0 280.2 reduce-scatter.2
  1100.6 829.2 reduce-scatter.4
  1933.0 38.8 all-reduce.3
  1973.4 1662.0 all-gather.26
